TPU v7x, 256 devices: a whole 4x4x8 slice. The times are simulated.
256 devices in a mesh: node: 16 (over x, y), tile: 16 (over z, core).
Axes of the slice: x: 4, y: 4, z: 8, core: 2. Of those that a mesh axis runs over, the one named last changes fastest.
Arguments:
- schur: float32 [16, 1536, 24576], P(None, 'tile', 'node'), may hold values from -0.0390625 to 0.0390625
- samples: float32 [16, 1536, 512], P(None, 'tile'), may hold values from -6 to 6
Outputs:
- leaf_basis: float32 [16, 1536, 512], P('node', 'tile')
- level_one: float32 [16, 512, 512], P('node', 'tile')
- level_two: float32 [16, 512, 512], P('node', 'tile')
All inputs are finite; a program needn't handle non-finite values.
Results may differ from a plain program's by a relative error of at most 0.00011.
Values sent between devices are 32-bit elements; how exact they have to be, the bound alone decides.
A program may use at most 128 MiB of HBM per device.

v0:
```python
import math
import jax
import jax.numpy as jnp
from jax import lax
from jax.sharding import PartitionSpec as P

HIGH = lax.Precision.HIGHEST


def swap(block, axis, mask):
    count = lax.axis_size(axis)
    return lax.ppermute(block, axis, [(low, low ^ mask) for low in range(count)])


def product(left, right):
    return jnp.dot(left, right, precision=HIGH, preferred_element_type=jnp.float32)


def transposed(left, right):
    return lax.dot_general(
        left, right, (((0,), (0,)), ((), ())), precision=HIGH, preferred_element_type=jnp.float32
    )


def inverse_lower(factor):
    eye = jnp.eye(factor.shape[0], dtype=factor.dtype)
    return jax.scipy.linalg.solve_triangular(factor, eye, lower=True)


def tile_bits():
    return [bit for bit in range(lax.axis_size("tile").bit_length() - 1)]


def halve(block):
    tile = lax.axis_index("tile")
    for bit in tile_bits():
        side = tile >> bit & 1
        half = block.shape[0] // 2
        keep = lax.dynamic_slice_in_dim(block, side * half, half, 0)
        send = lax.dynamic_slice_in_dim(block, (1 - side) * half, half, 0)
        block = keep + swap(send, "tile", 1 << bit)
    return block


def double(block, dim):
    tile = lax.axis_index("tile")
    for bit in reversed(tile_bits()):
        side = tile >> bit & 1
        other = swap(block, "tile", 1 << bit)
        block = jnp.where(
            side == 0,
            jnp.concatenate([block, other], axis=dim),
            jnp.concatenate([other, block], axis=dim),
        )
    return block


def chunk_rows(block, count):
    tile = lax.axis_index("tile")
    start = 0
    size = block.shape[0]
    for bit in tile_bits():
        size //= 2
        start = start + (tile >> bit & 1) * size
    return lax.dynamic_slice_in_dim(block, start, count, 0)


def on_device(schur, samples):
    leaves, slice_cols, leaf_rows = schur.shape
    rank_size = samples.shape[2]
    node = lax.axis_index("node")
    tile = lax.axis_index("tile")
    tile_count = lax.axis_size("tile")
    out_rows = rank_size // tile_count
    owned = lax.dynamic_index_in_dim(samples, node, 0, keepdims=False)
    keep = (jnp.arange(leaves, dtype=jnp.int32) != node)[:, None, None]
    masked = jnp.where(keep, samples, 0.0).reshape(leaves * slice_cols, rank_size)
    stacked = schur.reshape(leaves * slice_cols, leaf_rows)
    sample_rows = lax.psum_scatter(
        transposed(stacked, masked), "tile", scatter_dimension=0, tiled=True
    )
    both = lax.all_gather(jnp.concatenate([sample_rows, owned], axis=1), "tile", axis=0, tiled=True)
    local = both[:, :rank_size]
    omega = both[:, rank_size:]
    factor = jnp.linalg.cholesky(transposed(local, local))
    basis = product(local, inverse_lower(factor).T)
    reduced = transposed(basis, omega)
    basis_rows = lax.dynamic_slice_in_dim(basis, tile * slice_cols, slice_cols, 0)

    def meet(target):
        piece = lax.dynamic_index_in_dim(schur, target, 0, keepdims=False)
        return product(piece, basis)

    panel_one = product(basis_rows, reduced)
    sibling_rows = swap(panel_one, "node", 1)
    other_reduced = swap(reduced, "node", 1)
    near_meet = meet(jnp.bitwise_xor(node, 1))
    cousin_meet = meet(jnp.bitwise_xor(node, 2))
    further_meet = meet(jnp.bitwise_xor(node, 3))
    near_part = halve(transposed(near_meet, sibling_rows))
    sample_part = chunk_rows(factor.T, near_part.shape[0]) - near_part
    other_part = swap(sample_part, "node", 1)
    pair = double(jnp.stack([sample_part, other_part]), 1)
    parent_sample, other_sample = (pair[0], pair[1])
    parent_factor = jnp.linalg.cholesky(
        transposed(parent_sample, parent_sample) + transposed(other_sample, other_sample)
    )
    parent_inverse = inverse_lower(parent_factor).T
    transfer_own = product(parent_sample, parent_inverse)
    transfer_other = product(other_sample, parent_inverse)
    parent_reduced = transposed(transfer_own, reduced) + transposed(transfer_other, other_reduced)
    panel_two = product(basis_rows, product(transfer_own, parent_reduced))
    cousin_rows = swap(panel_two, "node", 2)
    further_rows = swap(panel_two, "node", 3)
    far_sum = transposed(cousin_meet, cousin_rows) + transposed(further_meet, further_rows)
    far_part = halve(transposed(transfer_own, far_sum))
    far_pair = far_part + swap(far_part, "node", 1)
    grand_part = chunk_rows(parent_factor.T, far_pair.shape[0]) - far_pair
    cousin_part = swap(grand_part, "node", 2)
    grand_pair = double(jnp.stack([grand_part, cousin_part]), 1)
    grand_sample, cousin_grand = (grand_pair[0], grand_pair[1])
    grand_factor = jnp.linalg.cholesky(
        transposed(grand_sample, grand_sample) + transposed(cousin_grand, cousin_grand)
    )
    grand_transfer = product(grand_sample, inverse_lower(grand_factor).T)
    leaf_out = (basis_rows * math.sqrt(leaf_rows))[None]
    one_rows = lax.dynamic_slice_in_dim(transfer_own, tile * out_rows, out_rows, 0)
    level_one = (one_rows * math.sqrt(2 * rank_size))[None]
    two_rows = product(one_rows, grand_transfer)
    level_two = (two_rows * (2.0 * math.sqrt(rank_size)))[None]
    return (leaf_out, level_one, level_two)


def solution(mesh):
    placed = (P(None, "tile", "node"), P(None, "tile", None))
    return jax.shard_map(
        on_device,
        mesh=mesh,
        in_specs=placed,
        out_specs=(P("node", "tile", None), P("node", "tile", None), P("node", "tile", None)),
        check_vma=False,
    )
```

profile of v0, /device:TPU:1, one launch (start us, length us, event | category | flops | bytes accessed | tf_op | source)
XLA Modules:
  0.0 900.6 jit_solution(1732461360240981253)
XLA Ops:
  7.2 18.4 %convolution_bitcast_fusion = f32[1536,512]{0,1:T(8,128)S(1)} fusion(f32[16,96,1536]{2,1,0:T(8,128)} %param.5, f32[16,96,512]{2,1,0:T(8,128)} %param.6, pred[16]{0:T(512)(128)(4,1)S(1)} %iota_compare_fusion.4), kind=kOutput, calls=%fused_computation.6 | convolution fusion | flops 14496301056 | bytes 15728656 | tf_op jit(solution)/shard_map/dot_general | solution.py:20
  29.4 60.6 %reduce-scatter.4.cloned.1.call-done = f32[96,512]{1,0:T(8,128)} async-done(((f32[1536,512]{1,0:T(8,128)}), f32[96,512]{1,0:T(8,128)}) %reduce-scatter.4.cloned.1.call-update) | async-done | bytes 196624
  92.2 48.0 %all-gather.2.cloned.1.call-done = f32[1536,1024]{1,0:T(8,128)} async-done(((f32[96,1024]{1,0:T(8,128)}), f32[1536,1024]{1,0:T(8,128)}) %all-gather.2.cloned.1.call-update) | async-done | bytes 6291472 | tf_op jit(solution)/shard_map/all_gather | solution.py:82
  149.7 11.7 %cholesky.374 = f32[128,128]{1,0:T(8,128)S(1)} custom-call(f32[128,128]{1,0:T(8,128)S(1)} %cholesky.586), custom_call_target="Cholesky" | custom-call | tf_op jit(solution)/shard_map/jit(cholesky)/cholesky | solution.py:85
  161.5 10.0 %custom-call.31 = f32[1,128,128]{1,2,0:T(8,128)S(1)} custom-call(f32[1,128,128]{2,1,0:T(8,128)S(1)} %get-tuple-element.91), custom_call_target="InvertDiagBlocksLowerTriangular" | custom-call | tf_op jit(solution)/shard_map/jit(cholesky)/cholesky | solution.py:85
  174.5 11.7 %cholesky.393 = f32[128,128]{1,0:T(8,128)S(1)} custom-call(f32[128,128]{1,0:T(8,128)S(1)} %cholesky.590), custom_call_target="Cholesky" | custom-call | tf_op jit(solution)/shard_map/jit(cholesky)/cholesky | solution.py:85
  197.7 11.7 %cholesky.414 = f32[128,128]{1,0:T(8,128)S(1)} custom-call(f32[128,128]{1,0:T(8,128)S(1)} %cholesky.595), custom_call_target="Cholesky" | custom-call | tf_op jit(solution)/shard_map/jit(cholesky)/cholesky | solution.py:85
  210.1 10.2 %custom-call.33 = f32[1,128,128]{1,2,0:T(8,128)S(1)} custom-call(f32[1,128,128]{2,1,0:T(8,128)S(1)} %get-tuple-element.85), custom_call_target="InvertDiagBlocksLowerTriangular" | custom-call | tf_op jit(solution)/shard_map/jit(cholesky)/cholesky | solution.py:85
  221.7 11.7 %cholesky.431 = f32[128,128]{1,0:T(8,128)S(1)} custom-call(f32[128,128]{1,0:T(8,128)S(1)} %convolution_subtract_fusion.17), custom_call_target="Cholesky" | custom-call | tf_op jit(solution)/shard_map/jit(cholesky)/cholesky | solution.py:85
  246.7 39.5 %custom-call.34 = f32[4,128,128]{1,2,0:T(8,128)S(1)} custom-call(f32[4,128,128]{2,1,0:T(8,128)S(1)} %get-tuple-element.25), custom_call_target="InvertDiagBlocksLowerTriangular" | custom-call | tf_op jit(solution)/shard_map/jit(_solve_triangular)/triangular_solve | solution.py:27
  327.8 12.6 %collective-permute-done.3 = f32[64,512]{0,1:T(8,128)} collective-permute-done((f32[64,512]{0,1:T(8,128)S(1)}, f32[64,512]{0,1:T(8,128)}, u32[]{:S(2)}, u32[]{:S(2)}) %collective-permute-start.3) | collective-permute-done | bytes 131104 | tf_op jit(solution)/shard_map/ppermute | solution.py:12
  344.9 14.9 %collective-permute-done.4 = f32[32,512]{0,1:T(8,128)} collective-permute-done((f32[32,512]{0,1:T(8,128)}, f32[32,512]{0,1:T(8,128)}, u32[]{:S(2)}, u32[]{:S(2)}) %collective-permute-start.4) | collective-permute-done | bytes 65568 | tf_op jit(solution)/shard_map/ppermute | solution.py:12
  378.5 14.7 %collective-permute-done.7 = f32[2,64,512]{2,1,0:T(8,128)} collective-permute-done((f32[2,64,512]{2,1,0:T(8,128)S(1)}, f32[2,64,512]{2,1,0:T(8,128)}, u32[]{:S(2)}, u32[]{:S(2)}) %collective-permute-start.7) | collective-permute-done | bytes 262176 | tf_op jit(solution)/shard_map/ppermute | solution.py:12
  395.1 13.3 %collective-permute-done.8 = f32[2,128,512]{2,1,0:T(8,128)} collective-permute-done((f32[2,128,512]{2,1,0:T(8,128)}, f32[2,128,512]{2,1,0:T(8,128)}, u32[]{:S(2)}, u32[]{:S(2)}) %collective-permute-start.8) | collective-permute-done | bytes 524320 | tf_op jit(solution)/shard_map/ppermute | solution.py:12
  430.1 11.7 %cholesky.446 = f32[128,128]{1,0:T(8,128)S(1)} custom-call(f32[128,128]{1,0:T(8,128)S(1)} %cholesky.599), custom_call_target="Cholesky" | custom-call | tf_op jit(solution)/shard_map/jit(cholesky)/cholesky | solution.py:105
  442.4 10.6 %custom-call.35 = f32[1,128,128]{1,2,0:T(8,128)} custom-call(f32[1,128,128]{2,1,0:T(8,128)S(1)} %get-tuple-element.81), custom_call_target="InvertDiagBlocksLowerTriangular" | custom-call | tf_op jit(solution)/shard_map/jit(cholesky)/cholesky | solution.py:105
  458.6 11.7 %cholesky.465 = f32[128,128]{1,0:T(8,128)S(1)} custom-call(f32[128,128]{1,0:T(8,128)S(1)} %cholesky.603), custom_call_target="Cholesky" | custom-call | tf_op jit(solution)/shard_map/jit(cholesky)/cholesky | solution.py:105
  487.0 12.3 %cholesky.486 = f32[128,128]{1,0:T(8,128)} custom-call(f32[128,128]{1,0:T(8,128)S(1)} %cholesky.608), custom_call_target="Cholesky" | custom-call | tf_op jit(solution)/shard_map/jit(cholesky)/cholesky | solution.py:105
  501.5 10.6 %custom-call.37 = f32[1,128,128]{1,2,0:T(8,128)} custom-call(f32[1,128,128]{2,1,0:T(8,128)S(1)} %get-tuple-element.75), custom_call_target="InvertDiagBlocksLowerTriangular" | custom-call | tf_op jit(solution)/shard_map/jit(cholesky)/cholesky | solution.py:105
  515.2 11.7 %cholesky.503 = f32[128,128]{1,0:T(8,128)S(1)} custom-call(f32[128,128]{1,0:T(8,128)S(1)} %convolution_subtract_fusion.16), custom_call_target="Cholesky" | custom-call | tf_op jit(solution)/shard_map/jit(cholesky)/cholesky | solution.py:105
  534.4 14.0 %while.7 = (s32[]{:T(128)}, f32[512,512]{1,0:T(8,128)}, s32[4,2]{0,1:T(2,128)S(1)}, f32[4,128,128]{2,1,0:T(8,128)}, s32[]{:T(128)}) while((s32[]{:T(128)}, f32[512,512]{1,0:T(8,128)}, s32[4,2]{0,1:T(2,128)S(1)}, f32[4,128,128]{2,1,0:T(8,128)}, s32[]{:T(128)}) %tuple.89), condition=%wide.while_cond.clone, body=%wide.while_body.clone.sunk | while | flops 2 | bytes 132705 | solution.py:27
  548.3 41.1 %custom-call.38 = f32[4,128,128]{1,2,0:T(8,128)} custom-call(f32[4,128,128]{2,1,0:T(8,128)} %get-tuple-element.26), custom_call_target="InvertDiagBlocksLowerTriangular" | custom-call | tf_op jit(solution)/shard_map/jit(_solve_triangular)/triangular_solve | solution.py:27
  635.8 14.5 %collective-permute-done.15 = f32[64,512]{0,1:T(8,128)S(1)} collective-permute-done((f32[64,512]{0,1:T(8,128)S(1)}, f32[64,512]{0,1:T(8,128)S(1)}, u32[]{:S(2)}, u32[]{:S(2)}) %collective-permute-start.15) | collective-permute-done | bytes 131104 | tf_op jit(solution)/shard_map/ppermute | solution.py:12
  652.3 14.7 %collective-permute-done.16 = f32[32,512]{0,1:T(8,128)S(1)} collective-permute-done((f32[32,512]{0,1:T(8,128)S(1)}, f32[32,512]{0,1:T(8,128)S(1)}, u32[]{:S(2)}, u32[]{:S(2)}) %collective-permute-start.16) | collective-permute-done | bytes 65568 | tf_op jit(solution)/shard_map/ppermute | solution.py:12
  693.2 13.6 %collective-permute-done.20 = f32[2,64,512]{2,1,0:T(8,128)S(1)} collective-permute-done((f32[2,64,512]{2,1,0:T(8,128)S(1)}, f32[2,64,512]{2,1,0:T(8,128)S(1)}, u32[]{:S(2)}, u32[]{:S(2)}) %collective-permute-start.20) | collective-permute-done | bytes 262176 | tf_op jit(solution)/shard_map/ppermute | solution.py:12
  707.0 12.1 %collective-permute-done.21 = f32[2,128,512]{2,1,0:T(8,128)S(1)} collective-permute-done((f32[2,128,512]{2,1,0:T(8,128)S(1)}, f32[2,128,512]{2,1,0:T(8,128)S(1)}, u32[]{:S(2)}, u32[]{:S(2)}) %collective-permute-start.21) | collective-permute-done | bytes 524320 | tf_op jit(solution)/shard_map/ppermute | solution.py:12
  735.5 11.7 %cholesky.518 = f32[128,128]{1,0:T(8,128)S(1)} custom-call(f32[128,128]{1,0:T(8,128)S(1)} %cholesky.612), custom_call_target="Cholesky" | custom-call | tf_op jit(solution)/shard_map/jit(cholesky)/cholesky | solution.py:122
  761.4 11.9 %cholesky.537 = f32[128,128]{1,0:T(8,128)S(1)} custom-call(f32[128,128]{1,0:T(8,128)S(1)} %cholesky.616), custom_call_target="Cholesky" | custom-call | tf_op jit(solution)/shard_map/jit(cholesky)/cholesky | solution.py:122
  787.5 11.7 %cholesky.558 = f32[128,128]{1,0:T(8,128)S(1)} custom-call(f32[128,128]{1,0:T(8,128)S(1)} %cholesky.621), custom_call_target="Cholesky" | custom-call | tf_op jit(solution)/shard_map/jit(cholesky)/cholesky | solution.py:122
  812.8 11.7 %cholesky.575 = f32[128,128]{1,0:T(8,128)S(1)} custom-call(f32[128,128]{1,0:T(8,128)S(1)} %convolution_subtract_fusion.15), custom_call_target="Cholesky" | custom-call | tf_op jit(solution)/shard_map/jit(cholesky)/cholesky | solution.py:122
  830.7 12.0 %while.8 = (s32[]{:T(128)}, f32[512,512]{1,0:T(8,128)}, s32[4,2]{0,1:T(2,128)S(1)}, f32[4,128,128]{2,1,0:T(8,128)S(1)}, s32[]{:T(128)}) while((s32[]{:T(128)}, f32[512,512]{1,0:T(8,128)}, s32[4,2]{0,1:T(2,128)S(1)}, f32[4,128,128]{2,1,0:T(8,128)S(1)}, s32[]{:T(128)}) %tuple.90), condition=%wide.while_cond.clone.1, body=%wide.while_body.clone.1.sunk | while | flops 2 | bytes 131181 | solution.py:27
  843.5 40.1 %custom-call.42 = f32[4,128,128]{1,2,0:T(8,128)S(1)} custom-call(f32[4,128,128]{2,1,0:T(8,128)} %copy-done.16), custom_call_target="InvertDiagBlocksLowerTriangular" | custom-call | tf_op jit(solution)/shard_map/jit(_solve_triangular)/triangular_solve | solution.py:27
  (279 shorter events, 344.6 us)
Async XLA Ops:
  7.2 82.9 %reduce-scatter.4.cloned.1.call-start = ((), (), s32[]{:S(2)}) async-start(), calls=%async_computation.2 | async-start | bytes 3342336
  28.1 112.1 %all-gather.2.cloned.1.call-start = ((), (), s32[]{:S(2)}) async-start(), calls=%async_computation.1 | async-start | bytes 6684672 | tf_op jit(solution)/shard_map/all_gather | solution.py:82
  92.2 196.1 %copy-start.3 = (f32[512,512]{1,0:T(8,128)}, f32[512,512]{1,0:T(8,128)S(1)}, u32[]{:S(2)}) copy-start(f32[512,512]{1,0:T(8,128)S(1)} %fusion.32) | copy-start | bytes 3145732
  288.9 7.7 slice-start
  289.4 7.3 slice-start.1
  302.1 8.1 copy-start.5
  302.9 6.3 collective-permute-start
  311.4 2.9 collective-permute-start.1
  316.5 7.7 collective-permute-start.2
  326.1 14.3 %collective-permute-start.3 = (f32[64,512]{0,1:T(8,128)S(1)}, f32[64,512]{0,1:T(8,128)}, u32[]{:S(2)}, u32[]{:S(2)}) collective-permute-start(f32[64,512]{0,1:T(8,128)S(1)} %constant_dynamic-slice_fusion.8), channel_id=1, source_target_pairs={{0,4},{1,5},{2,6},{3,7},{4,0},{5,1},{6,2},{7,3},{8,12},{9,13},{10,... | collective-permute-start | bytes 393224 | tf_op jit(solution)/shard_map/ppermute | solution.py:12
  342.3 17.4 %collective-permute-start.4 = (f32[32,512]{0,1:T(8,128)}, f32[32,512]{0,1:T(8,128)}, u32[]{:S(2)}, u32[]{:S(2)}) collective-permute-start(f32[32,512]{0,1:T(8,128)} %constant_dynamic-slice_fusion.7), channel_id=1, source_target_pairs={{0,8},{1,9},{2,10},{3,11},{4,12},{5,13},{6,14},{7,15},{8,0},{9,1},... | collective-permute-start | bytes 196616 | tf_op jit(solution)/shard_map/ppermute | solution.py:12
  361.7 7.6 collective-permute-start.5
  369.4 7.9 collective-permute-start.6
  378.4 14.8 %collective-permute-start.7 = (f32[2,64,512]{2,1,0:T(8,128)S(1)}, f32[2,64,512]{2,1,0:T(8,128)}, u32[]{:S(2)}, u32[]{:S(2)}) collective-permute-start(f32[2,64,512]{2,1,0:T(8,128)S(1)} %maximum_select_fusion.6), channel_id=1, source_target_pairs={{0,4},{1,5},{2,6},{3,7},{4,0},{5,1},{6,2},{7,3},{8,12},{9,13},{10,... | collective-permute-start | bytes 786440 | tf_op jit(solution)/shard_map/ppermute | solution.py:12
  395.1 13.3 %collective-permute-start.8 = (f32[2,128,512]{2,1,0:T(8,128)}, f32[2,128,512]{2,1,0:T(8,128)}, u32[]{:S(2)}, u32[]{:S(2)}) collective-permute-start(f32[2,128,512]{2,1,0:T(8,128)} %maximum_select_fusion.4), channel_id=1, source_target_pairs={{0,2},{1,3},{2,0},{3,1},{4,6},{5,7},{6,4},{7,5},{8,10},{9,11},{10,... | collective-permute-start | bytes 1572872 | tf_op jit(solution)/shard_map/ppermute | solution.py:12
  411.2 6.0 collective-permute-start.9
  412.6 190.8 %collective-permute-start.10 = (f32[512,512]{1,0:T(8,128)}, f32[512,512]{1,0:T(8,128)}, u32[]{:S(2)}, u32[]{:S(2)}) collective-permute-start(f32[512,512]{1,0:T(8,128)} %copy-done.5), channel_id=1, source_target_pairs={{0,16},{16,0},{32,48},{48,32},{64,80},{80,64},{96,112},{112,96},{1... | collective-permute-start | bytes 3145736 | tf_op jit(solution)/shard_map/ppermute | solution.py:12
  589.4 8.2 copy-start.1
  601.4 21.3 %copy-start.2 = (f32[512,512]{1,0:T(8,128)}, f32[512,512]{1,0:T(8,128)S(1)}, u32[]{:S(2)}) copy-start(f32[512,512]{1,0:T(8,128)S(1)} %fusion.33) | copy-start | bytes 3145732
  609.3 7.5 collective-permute-start.12
  614.2 7.5 collective-permute-start.11
  624.7 3.0 collective-permute-start.13
  627.9 7.6 collective-permute-start.14
  635.7 14.6 %collective-permute-start.15 = (f32[64,512]{0,1:T(8,128)S(1)}, f32[64,512]{0,1:T(8,128)S(1)}, u32[]{:S(2)}, u32[]{:S(2)}) collective-permute-start(f32[64,512]{0,1:T(8,128)S(1)} %constant_dynamic-slice_fusion.4), channel_id=1, source_target_pairs={{0,4},{1,5},{2,6},{3,7},{4,0},{5,1},{6,2},{7,3},{8,12},{9,13},{10,... | collective-permute-start | bytes 393224 | tf_op jit(solution)/shard_map/ppermute | solution.py:12
  650.5 16.4 %collective-permute-start.16 = (f32[32,512]{0,1:T(8,128)S(1)}, f32[32,512]{0,1:T(8,128)S(1)}, u32[]{:S(2)}, u32[]{:S(2)}) collective-permute-start(f32[32,512]{0,1:T(8,128)S(1)} %constant_dynamic-slice_fusion.3), channel_id=1, source_target_pairs={{0,8},{1,9},{2,10},{3,11},{4,12},{5,13},{6,14},{7,15},{8,0},{9,1},... | collective-permute-start | bytes 196616 | tf_op jit(solution)/shard_map/ppermute | solution.py:12
  667.1 7.5 collective-permute-start.17
  675.6 8.2 collective-permute-start.18
  684.9 7.8 collective-permute-start.19
  692.7 14.1 %collective-permute-start.20 = (f32[2,64,512]{2,1,0:T(8,128)S(1)}, f32[2,64,512]{2,1,0:T(8,128)S(1)}, u32[]{:S(2)}, u32[]{:S(2)}) collective-permute-start(f32[2,64,512]{2,1,0:T(8,128)S(1)} %maximum_select_fusion.7), channel_id=1, source_target_pairs={{0,4},{1,5},{2,6},{3,7},{4,0},{5,1},{6,2},{7,3},{8,12},{9,13},{10,... | collective-permute-start | bytes 786440 | tf_op jit(solution)/shard_map/ppermute | solution.py:12
  706.9 12.2 %collective-permute-start.21 = (f32[2,128,512]{2,1,0:T(8,128)S(1)}, f32[2,128,512]{2,1,0:T(8,128)S(1)}, u32[]{:S(2)}, u32[]{:S(2)}) collective-permute-start(f32[2,128,512]{2,1,0:T(8,128)S(1)} %maximum_select_fusion.5), channel_id=1, source_target_pairs={{0,2},{1,3},{2,0},{3,1},{4,6},{5,7},{6,4},{7,5},{8,10},{9,11},{10,... | collective-permute-start | bytes 1572872 | tf_op jit(solution)/shard_map/ppermute | solution.py:12
  720.2 4.9 collective-permute-start.22
  760.1 123.5 %copy-start.4 = (f32[512,512]{1,0:T(8,128)S(1)}, f32[512,512]{1,0:T(8,128)}, u32[]{:S(2)}) copy-start(f32[512,512]{1,0:T(8,128)} %copy-done.3) | copy-start | bytes 3145732
  (12 other events, 20.4 us)
Sparse Core Ops, SparseCore 0:
  28.2 61.7 reduce-scatter.3
  92.2 47.9 all-gather.1
where the time goes:
time: 906 us; the launch traced here: 901 us
  other arithmetic  396 us (44%)
  waiting for transfers between devices  276 us (30%)
  matrix products  118 us (13%)
  local copies, waits for them, and re-layouts  60.8 us (7%)
  starting transfers between devices  26.4 us (3%)
  between operations  23.1 us (3%)
    ppermute x23, waiting for transfers between devices, swap(): lax.ppermute(block, axis, [(low, low ^ mask) for low in range(count)])  167 us
    another operation x7, other arithmetic, inverse_lower(): return jax.scipy.linalg.solve_triangular(factor, eye, lower=True)  127 us
    another operation x15, other arithmetic, on_device(): jnp.linalg.cholesky(transposed(parent_sample, parent_sample) + transposed...  83.9 us
    another operation x15, other arithmetic, on_device(): jnp.linalg.cholesky(transposed(grand_sample, grand_sample) + transposed(c...  81.2 us
    another operation x14, other arithmetic, on_device(): factor = jnp.linalg.cholesky(transposed(local, local))  79 us
    unnamed x3, waiting for transfers between devices  60.7 us
    dot_general x13, matrix products, transposed(): lax.dot_general(left, right, (((0,), (0,)), ((), ())), precision=HIGH, pr...  50.4 us
    all_gather x1, waiting for transfers between devices, on_device(): lax.all_gather(jnp.concatenate([sample_rows, owned], axis=1), 'tile', axi...  48 us
  transfers between devices with their start and end apart: 25, of which 23 were waited for; matrix products, arithmetic and copies ran while one was open for 22% of the time, Pallas kernels for 0%

commit v1 on v0

--- a/solution.py
+++ b/solution.py
@@ -79,7 +79,15 @@
     sample_rows = lax.psum_scatter(
         transposed(stacked, masked), "tile", scatter_dimension=0, tiled=True
     )
-    both = lax.all_gather(jnp.concatenate([sample_rows, owned], axis=1), "tile", axis=0, tiled=True)
+    both = jnp.concatenate(
+        lax.all_to_all(
+            jnp.stack([jnp.concatenate([sample_rows, owned], axis=1)] * lax.axis_size("tile")),
+            "tile",
+            0,
+            0,
+        ),
+        axis=0,
+    )
     local = both[:, :rank_size]
     omega = both[:, rank_size:]
     factor = jnp.linalg.cholesky(transposed(local, local))

time: 906 us -> 1000 us (1.10)
  waiting for transfers between devices: 276 us -> 353 us
  starting transfers between devices: 26.4 us -> 42.5 us
    all_to_all x0 -> x1, waiting for transfers between devices: none -> 138 us  [on_device(): lax.all_to_all(jnp.stack([jnp.concatenate([sample_rows, owned], axis=1)]...]
    all_gather x1 -> x0, waiting for transfers between devices: 48 us -> none  [on_device(): lax.all_gather(jnp.concatenate([sample_rows, owned], axis=1), 'tile', axi...]
    ppermute x23, waiting for transfers between devices: 167 us -> 154 us  [swap(): lax.ppermute(block, axis, [(low, low ^ mask) for low in range(count)])]
    unnamed x3 -> x2, waiting for transfers between devices: 60.7 us -> 60.9 us
  transfers between devices with their start and end apart: 25 -> 25, of which waited for: 23 -> 23; matrix products, arithmetic and copies ran while one was open for 22% -> 20% of each run, Pallas kernels for 0% -> 0%
where the time goes in v1:
time: 1000 us; the launch traced here: 997 us
  other arithmetic  396 us (40%)
  waiting for transfers between devices  353 us (35%)
  matrix products  120 us (12%)
  local copies, waits for them, and re-layouts  63 us (6%)
  starting transfers between devices  42.5 us (4%)
  between operations  22.9 us (2%)
    ppermute x23, waiting for transfers between devices, swap(): lax.ppermute(block, axis, [(low, low ^ mask) for low in range(count)])  154 us
    all_to_all x1, waiting for transfers between devices, on_device(): lax.all_to_all(jnp.stack([jnp.concatenate([sample_rows, owned], axis=1)]...  138 us
    another operation x7, other arithmetic, inverse_lower(): return jax.scipy.linalg.solve_triangular(factor, eye, lower=True)  127 us
    another operation x15, other arithmetic, on_device(): jnp.linalg.cholesky(transposed(parent_sample, parent_sample) + transposed...  84.1 us
    another operation x15, other arithmetic, on_device(): jnp.linalg.cholesky(transposed(grand_sample, grand_sample) + transposed(c...  81.4 us
    another operation x14, other arithmetic, on_device(): factor = jnp.linalg.cholesky(transposed(local, local))  78.6 us
    unnamed x2, waiting for transfers between devices  60.9 us
    dot_general x13, matrix products, transposed(): lax.dot_general(left, right, (((0,), (0,)), ((), ())), precision=HIGH, pr...  52.2 us
  transfers between devices with their start and end apart: 25, of which 23 were waited for; matrix products, arithmetic and copies ran while one was open for 20% of the time, Pallas kernels for 0%

profile of v1, /device:TPU:1, one launch (start us, length us, event | category | flops | bytes accessed | tf_op | source)
XLA Modules:
  0.0 997.5 jit_solution(5022567667047509280)
XLA Ops:
  7.2 18.4 %convolution_bitcast_fusion = f32[1536,512]{0,1:T(8,128)S(1)} fusion(f32[16,96,1536]{2,1,0:T(8,128)} %param.5, f32[16,96,512]{2,1,0:T(8,128)} %param.6, pred[16]{0:T(512)(128)(4,1)S(1)} %iota_compare_fusion.4), kind=kOutput, calls=%fused_computation.6 | convolution fusion | flops 14496301056 | bytes 15728656 | tf_op jit(solution)/shard_map/dot_general | solution.py:20
  29.2 60.9 %reduce-scatter.4.cloned.1.call-done = f32[96,512]{1,0:T(8,128)} async-done(((f32[1536,512]{1,0:T(8,128)}), f32[96,512]{1,0:T(8,128)}) %reduce-scatter.4.cloned.1.call-update) | async-done | bytes 196624
  103.4 138.0 %all-to-all-done = f32[16,96,1024]{2,1,0:T(8,128)} async-done(((f32[16,96,1024]{2,1,0:T(8,128)}), f32[16,96,1024]{2,1,0:T(8,128)}, u32[]{:S(2)}, u32[]{:S(2)}) %all-to-all-start) | async-done | bytes 6291488 | tf_op jit(solution)/shard_map/all_to_all | solution.py:83
  251.0 11.7 %cholesky.374 = f32[128,128]{1,0:T(8,128)S(1)} custom-call(f32[128,128]{1,0:T(8,128)S(1)} %cholesky.586), custom_call_target="Cholesky" | custom-call | tf_op jit(solution)/shard_map/jit(cholesky)/cholesky | solution.py:93
  275.8 11.7 %cholesky.393 = f32[128,128]{1,0:T(8,128)S(1)} custom-call(f32[128,128]{1,0:T(8,128)S(1)} %cholesky.590), custom_call_target="Cholesky" | custom-call | tf_op jit(solution)/shard_map/jit(cholesky)/cholesky | solution.py:93
  298.9 11.7 %cholesky.414 = f32[128,128]{1,0:T(8,128)S(1)} custom-call(f32[128,128]{1,0:T(8,128)S(1)} %cholesky.595), custom_call_target="Cholesky" | custom-call | tf_op jit(solution)/shard_map/jit(cholesky)/cholesky | solution.py:93
  311.4 10.0 %custom-call.33 = f32[1,128,128]{1,2,0:T(8,128)S(1)} custom-call(f32[1,128,128]{2,1,0:T(8,128)S(1)} %get-tuple-element.85), custom_call_target="InvertDiagBlocksLowerTriangular" | custom-call | tf_op jit(solution)/shard_map/jit(cholesky)/cholesky | solution.py:93
  322.8 11.7 %cholesky.431 = f32[128,128]{1,0:T(8,128)S(1)} custom-call(f32[128,128]{1,0:T(8,128)S(1)} %convolution_subtract_fusion.17), custom_call_target="Cholesky" | custom-call | tf_op jit(solution)/shard_map/jit(cholesky)/cholesky | solution.py:93
  347.7 39.7 %custom-call.34 = f32[4,128,128]{1,2,0:T(8,128)S(1)} custom-call(f32[4,128,128]{2,1,0:T(8,128)S(1)} %get-tuple-element.25), custom_call_target="InvertDiagBlocksLowerTriangular" | custom-call | tf_op jit(solution)/shard_map/jit(_solve_triangular)/triangular_solve | solution.py:27
  431.4 11.6 %collective-permute-done.3 = f32[64,512]{0,1:T(8,128)} collective-permute-done((f32[64,512]{0,1:T(8,128)S(1)}, f32[64,512]{0,1:T(8,128)}, u32[]{:S(2)}, u32[]{:S(2)}) %collective-permute-start.3) | collective-permute-done | bytes 131104 | tf_op jit(solution)/shard_map/ppermute | solution.py:12
  448.5 14.2 %collective-permute-done.4 = f32[32,512]{0,1:T(8,128)} collective-permute-done((f32[32,512]{0,1:T(8,128)}, f32[32,512]{0,1:T(8,128)}, u32[]{:S(2)}, u32[]{:S(2)}) %collective-permute-start.4) | collective-permute-done | bytes 65568 | tf_op jit(solution)/shard_map/ppermute | solution.py:12
  480.9 12.1 %collective-permute-done.7 = f32[2,64,512]{2,1,0:T(8,128)} collective-permute-done((f32[2,64,512]{2,1,0:T(8,128)S(1)}, f32[2,64,512]{2,1,0:T(8,128)}, u32[]{:S(2)}, u32[]{:S(2)}) %collective-permute-start.7) | collective-permute-done | bytes 262176 | tf_op jit(solution)/shard_map/ppermute | solution.py:12
  494.9 12.2 %collective-permute-done.8 = f32[2,128,512]{2,1,0:T(8,128)} collective-permute-done((f32[2,128,512]{2,1,0:T(8,128)}, f32[2,128,512]{2,1,0:T(8,128)}, u32[]{:S(2)}, u32[]{:S(2)}) %collective-permute-start.8) | collective-permute-done | bytes 524320 | tf_op jit(solution)/shard_map/ppermute | solution.py:12
  529.4 11.7 %cholesky.446 = f32[128,128]{1,0:T(8,128)S(1)} custom-call(f32[128,128]{1,0:T(8,128)S(1)} %cholesky.599), custom_call_target="Cholesky" | custom-call | tf_op jit(solution)/shard_map/jit(cholesky)/cholesky | solution.py:113
  541.8 10.8 %custom-call.35 = f32[1,128,128]{1,2,0:T(8,128)} custom-call(f32[1,128,128]{2,1,0:T(8,128)S(1)} %get-tuple-element.81), custom_call_target="InvertDiagBlocksLowerTriangular" | custom-call | tf_op jit(solution)/shard_map/jit(cholesky)/cholesky | solution.py:113
  558.2 11.7 %cholesky.465 = f32[128,128]{1,0:T(8,128)S(1)} custom-call(f32[128,128]{1,0:T(8,128)S(1)} %cholesky.603), custom_call_target="Cholesky" | custom-call | tf_op jit(solution)/shard_map/jit(cholesky)/cholesky | solution.py:113
  586.6 12.3 %cholesky.486 = f32[128,128]{1,0:T(8,128)} custom-call(f32[128,128]{1,0:T(8,128)S(1)} %cholesky.608), custom_call_target="Cholesky" | custom-call | tf_op jit(solution)/shard_map/jit(cholesky)/cholesky | solution.py:113
  601.1 10.6 %custom-call.37 = f32[1,128,128]{1,2,0:T(8,128)} custom-call(f32[1,128,128]{2,1,0:T(8,128)S(1)} %get-tuple-element.75), custom_call_target="InvertDiagBlocksLowerTriangular" | custom-call | tf_op jit(solution)/shard_map/jit(cholesky)/cholesky | solution.py:113
  614.8 11.7 %cholesky.503 = f32[128,128]{1,0:T(8,128)S(1)} custom-call(f32[128,128]{1,0:T(8,128)S(1)} %convolution_subtract_fusion.16), custom_call_target="Cholesky" | custom-call | tf_op jit(solution)/shard_map/jit(cholesky)/cholesky | solution.py:113
  633.9 14.0 %while.7 = (s32[]{:T(128)}, f32[512,512]{1,0:T(8,128)}, s32[4,2]{0,1:T(2,128)S(1)}, f32[4,128,128]{2,1,0:T(8,128)}, s32[]{:T(128)}) while((s32[]{:T(128)}, f32[512,512]{1,0:T(8,128)}, s32[4,2]{0,1:T(2,128)S(1)}, f32[4,128,128]{2,1,0:T(8,128)}, s32[]{:T(128)}) %tuple.87), condition=%wide.while_cond.clone, body=%wide.while_body.clone.sunk | while | flops 2 | bytes 132705 | solution.py:27
  647.8 40.9 %custom-call.38 = f32[4,128,128]{1,2,0:T(8,128)} custom-call(f32[4,128,128]{2,1,0:T(8,128)} %get-tuple-element.26), custom_call_target="InvertDiagBlocksLowerTriangular" | custom-call | tf_op jit(solution)/shard_map/jit(_solve_triangular)/triangular_solve | solution.py:27
  737.1 12.7 %collective-permute-done.15 = f32[64,512]{0,1:T(8,128)S(1)} collective-permute-done((f32[64,512]{0,1:T(8,128)S(1)}, f32[64,512]{0,1:T(8,128)S(1)}, u32[]{:S(2)}, u32[]{:S(2)}) %collective-permute-start.15) | collective-permute-done | bytes 131104 | tf_op jit(solution)/shard_map/ppermute | solution.py:12
  752.7 14.7 %collective-permute-done.16 = f32[32,512]{0,1:T(8,128)S(1)} collective-permute-done((f32[32,512]{0,1:T(8,128)S(1)}, f32[32,512]{0,1:T(8,128)S(1)}, u32[]{:S(2)}, u32[]{:S(2)}) %collective-permute-start.16) | collective-permute-done | bytes 65568 | tf_op jit(solution)/shard_map/ppermute | solution.py:12
  793.4 10.8 %collective-permute-done.20 = f32[2,64,512]{2,1,0:T(8,128)S(1)} collective-permute-done((f32[2,64,512]{2,1,0:T(8,128)S(1)}, f32[2,64,512]{2,1,0:T(8,128)S(1)}, u32[]{:S(2)}, u32[]{:S(2)}) %collective-permute-start.20) | collective-permute-done | bytes 262176 | tf_op jit(solution)/shard_map/ppermute | solution.py:12
  804.4 11.8 %collective-permute-done.21 = f32[2,128,512]{2,1,0:T(8,128)S(1)} collective-permute-done((f32[2,128,512]{2,1,0:T(8,128)S(1)}, f32[2,128,512]{2,1,0:T(8,128)S(1)}, u32[]{:S(2)}, u32[]{:S(2)}) %collective-permute-start.21) | collective-permute-done | bytes 524320 | tf_op jit(solution)/shard_map/ppermute | solution.py:12
  832.9 11.7 %cholesky.518 = f32[128,128]{1,0:T(8,128)S(1)} custom-call(f32[128,128]{1,0:T(8,128)S(1)} %cholesky.612), custom_call_target="Cholesky" | custom-call | tf_op jit(solution)/shard_map/jit(cholesky)/cholesky | solution.py:130
  858.8 12.1 %cholesky.537 = f32[128,128]{1,0:T(8,128)S(1)} custom-call(f32[128,128]{1,0:T(8,128)S(1)} %cholesky.616), custom_call_target="Cholesky" | custom-call | tf_op jit(solution)/shard_map/jit(cholesky)/cholesky | solution.py:130
  885.0 11.7 %cholesky.558 = f32[128,128]{1,0:T(8,128)S(1)} custom-call(f32[128,128]{1,0:T(8,128)S(1)} %cholesky.621), custom_call_target="Cholesky" | custom-call | tf_op jit(solution)/shard_map/jit(cholesky)/cholesky | solution.py:130
  898.0 9.9 custom-call.41
  910.2 11.7 %cholesky.575 = f32[128,128]{1,0:T(8,128)S(1)} custom-call(f32[128,128]{1,0:T(8,128)S(1)} %convolution_subtract_fusion.15), custom_call_target="Cholesky" | custom-call | tf_op jit(solution)/shard_map/jit(cholesky)/cholesky | solution.py:130
  928.2 11.5 %while.8 = (s32[]{:T(128)}, f32[512,512]{1,0:T(8,128)}, s32[4,2]{0,1:T(2,128)S(1)}, f32[4,128,128]{2,1,0:T(8,128)S(1)}, s32[]{:T(128)}) while((s32[]{:T(128)}, f32[512,512]{1,0:T(8,128)}, s32[4,2]{0,1:T(2,128)S(1)}, f32[4,128,128]{2,1,0:T(8,128)S(1)}, s32[]{:T(128)}) %tuple.88), condition=%wide.while_cond.clone.1, body=%wide.while_body.clone.1.sunk | while | flops 2 | bytes 131181 | solution.py:27
  940.4 40.1 %custom-call.42 = f32[4,128,128]{1,2,0:T(8,128)S(1)} custom-call(f32[4,128,128]{2,1,0:T(8,128)} %copy-done.16), custom_call_target="InvertDiagBlocksLowerTriangular" | custom-call | tf_op jit(solution)/shard_map/jit(_solve_triangular)/triangular_solve | solution.py:27
  (274 shorter events, 361.3 us)
Async XLA Ops:
  7.2 82.9 %reduce-scatter.4.cloned.1.call-start = ((), (), s32[]{:S(2)}) async-start(), calls=%async_computation.2 | async-start | bytes 3342336
  94.8 146.7 %all-to-all-start = ((f32[16,96,1024]{2,1,0:T(8,128)}), f32[16,96,1024]{2,1,0:T(8,128)}, u32[]{:S(2)}, u32[]{:S(2)}) async-start(f32[16,96,1024]{2,1,0:T(8,128)} %stack.14), calls=%async_computation | async-start | bytes 12582912 | tf_op jit(solution)/shard_map/all_to_all | solution.py:83
  103.4 286.1 %copy-start.3 = (f32[512,512]{1,0:T(8,128)}, f32[512,512]{1,0:T(8,128)S(1)}, u32[]{:S(2)}) copy-start(f32[512,512]{1,0:T(8,128)S(1)} %fusion.32) | copy-start | bytes 3145732
  404.9 7.4 copy-start.5
  405.7 5.6 collective-permute-start
  413.5 3.7 collective-permute-start.1
  419.3 7.7 collective-permute-start.2
  428.9 14.1 %collective-permute-start.3 = (f32[64,512]{0,1:T(8,128)S(1)}, f32[64,512]{0,1:T(8,128)}, u32[]{:S(2)}, u32[]{:S(2)}) collective-permute-start(f32[64,512]{0,1:T(8,128)S(1)} %constant_dynamic-slice_fusion.8), channel_id=1, source_target_pairs={{0,4},{1,5},{2,6},{3,7},{4,0},{5,1},{6,2},{7,3},{8,12},{9,13},{10,... | collective-permute-start | bytes 393224 | tf_op jit(solution)/shard_map/ppermute | solution.py:12
  444.9 17.7 %collective-permute-start.4 = (f32[32,512]{0,1:T(8,128)}, f32[32,512]{0,1:T(8,128)}, u32[]{:S(2)}, u32[]{:S(2)}) collective-permute-start(f32[32,512]{0,1:T(8,128)} %constant_dynamic-slice_fusion.7), channel_id=1, source_target_pairs={{0,8},{1,9},{2,10},{3,11},{4,12},{5,13},{6,14},{7,15},{8,0},{9,1},... | collective-permute-start | bytes 196616 | tf_op jit(solution)/shard_map/ppermute | solution.py:12
  464.6 7.2 collective-permute-start.5
  471.8 7.9 collective-permute-start.6
  480.8 12.2 %collective-permute-start.7 = (f32[2,64,512]{2,1,0:T(8,128)S(1)}, f32[2,64,512]{2,1,0:T(8,128)}, u32[]{:S(2)}, u32[]{:S(2)}) collective-permute-start(f32[2,64,512]{2,1,0:T(8,128)S(1)} %maximum_select_fusion.6), channel_id=1, source_target_pairs={{0,4},{1,5},{2,6},{3,7},{4,0},{5,1},{6,2},{7,3},{8,12},{9,13},{10,... | collective-permute-start | bytes 786440 | tf_op jit(solution)/shard_map/ppermute | solution.py:12
  494.9 12.2 %collective-permute-start.8 = (f32[2,128,512]{2,1,0:T(8,128)}, f32[2,128,512]{2,1,0:T(8,128)}, u32[]{:S(2)}, u32[]{:S(2)}) collective-permute-start(f32[2,128,512]{2,1,0:T(8,128)} %maximum_select_fusion.4), channel_id=1, source_target_pairs={{0,2},{1,3},{2,0},{3,1},{4,6},{5,7},{6,4},{7,5},{8,10},{9,11},{10,... | collective-permute-start | bytes 1572872 | tf_op jit(solution)/shard_map/ppermute | solution.py:12
  509.9 6.6 collective-permute-start.9
  512.3 190.4 %collective-permute-start.10 = (f32[512,512]{1,0:T(8,128)}, f32[512,512]{1,0:T(8,128)}, u32[]{:S(2)}, u32[]{:S(2)}) collective-permute-start(f32[512,512]{1,0:T(8,128)} %copy-done.5), channel_id=1, source_target_pairs={{0,16},{16,0},{32,48},{48,32},{64,80},{80,64},{96,112},{112,96},{1... | collective-permute-start | bytes 3145736 | tf_op jit(solution)/shard_map/ppermute | solution.py:12
  688.8 5.7 copy-start.14
  688.8 8.2 copy-start.1
  697.0 3.8 copy-start.6
  700.8 21.8 %copy-start.2 = (f32[512,512]{1,0:T(8,128)}, f32[512,512]{1,0:T(8,128)S(1)}, u32[]{:S(2)}) copy-start(f32[512,512]{1,0:T(8,128)S(1)} %fusion.33) | copy-start | bytes 3145732
  709.0 7.5 collective-permute-start.12
  714.0 7.5 collective-permute-start.11
  724.6 3.0 collective-permute-start.13
  727.7 7.6 collective-permute-start.14
  735.5 14.4 %collective-permute-start.15 = (f32[64,512]{0,1:T(8,128)S(1)}, f32[64,512]{0,1:T(8,128)S(1)}, u32[]{:S(2)}, u32[]{:S(2)}) collective-permute-start(f32[64,512]{0,1:T(8,128)S(1)} %constant_dynamic-slice_fusion.4), channel_id=1, source_target_pairs={{0,4},{1,5},{2,6},{3,7},{4,0},{5,1},{6,2},{7,3},{8,12},{9,13},{10,... | collective-permute-start | bytes 393224 | tf_op jit(solution)/shard_map/ppermute | solution.py:12
  750.1 17.2 %collective-permute-start.16 = (f32[32,512]{0,1:T(8,128)S(1)}, f32[32,512]{0,1:T(8,128)S(1)}, u32[]{:S(2)}, u32[]{:S(2)}) collective-permute-start(f32[32,512]{0,1:T(8,128)S(1)} %constant_dynamic-slice_fusion.3), channel_id=1, source_target_pairs={{0,8},{1,9},{2,10},{3,11},{4,12},{5,13},{6,14},{7,15},{8,0},{9,1},... | collective-permute-start | bytes 196616 | tf_op jit(solution)/shard_map/ppermute | solution.py:12
  767.5 7.5 collective-permute-start.17
  776.0 8.2 collective-permute-start.18
  785.3 7.8 collective-permute-start.19
  793.1 11.1 %collective-permute-start.20 = (f32[2,64,512]{2,1,0:T(8,128)S(1)}, f32[2,64,512]{2,1,0:T(8,128)S(1)}, u32[]{:S(2)}, u32[]{:S(2)}) collective-permute-start(f32[2,64,512]{2,1,0:T(8,128)S(1)} %maximum_select_fusion.7), channel_id=1, source_target_pairs={{0,4},{1,5},{2,6},{3,7},{4,0},{5,1},{6,2},{7,3},{8,12},{9,13},{10,... | collective-permute-start | bytes 786440 | tf_op jit(solution)/shard_map/ppermute | solution.py:12
  804.3 11.9 %collective-permute-start.21 = (f32[2,128,512]{2,1,0:T(8,128)S(1)}, f32[2,128,512]{2,1,0:T(8,128)S(1)}, u32[]{:S(2)}, u32[]{:S(2)}) collective-permute-start(f32[2,128,512]{2,1,0:T(8,128)S(1)} %maximum_select_fusion.5), channel_id=1, source_target_pairs={{0,2},{1,3},{2,0},{3,1},{4,6},{5,7},{6,4},{7,5},{8,10},{9,11},{10,... | collective-permute-start | bytes 1572872 | tf_op jit(solution)/shard_map/ppermute | solution.py:12
  817.3 5.1 collective-permute-start.22
  857.5 123.1 %copy-start.4 = (f32[512,512]{1,0:T(8,128)S(1)}, f32[512,512]{1,0:T(8,128)}, u32[]{:S(2)}) copy-start(f32[512,512]{1,0:T(8,128)} %copy-done.3) | copy-start | bytes 3145732
  (10 other events, 11.0 us)
Sparse Core Ops, SparseCore 0:
  28.2 61.7 reduce-scatter.3
